TPU v7x, 128 devices: a whole 4x4x4 slice. The times are simulated.
128 devices in a mesh: bin: 16 (over z_lo, x, core), trk: 8 (over y, z_hi).
Axes of the slice: x: 4, y: 4, z: 4 (z_hi: 2, z_lo: 2; z = z_hi * 2 + z_lo), core: 2. Of those that a mesh axis runs over, the one named last changes fastest.
Arguments:
- trunk: bfloat16 [8192, 1536], P(('bin', 'trk')), may hold values from -6 to 6
- norm_gain: float32 [1536], replicated, may hold values from 0.1 to 1.9
- w_query: bfloat16 [1536, 1024], replicated, may hold values from -0.4375 to 0.4375
- w_kv: bfloat16 [1536, 256], replicated, may hold values from -0.15625 to 0.15625
- w_out: bfloat16 [1024, 1536], replicated, may hold values from -0.1875 to 0.1875
- w_up: bfloat16 [1536, 768], replicated, may hold values from -0.15625 to 0.15625
- skip: bfloat16 [32768, 768], P(('bin', 'trk')), may hold values from -6 to 6
- conv_w: bfloat16 [5, 768, 768], replicated, may hold values from -0.09375 to 0.09375
- head_w: bfloat16 [768, 6144], P(None, 'trk'), may hold values from -0.21875 to 0.21875
- head_bias: float32 [6144], P('trk'), may hold values from -4 to 4
- targets: bfloat16 [32768, 6144], P('bin', 'trk'), may hold values from 0.049804688 to 4
- missing: int32 [8192], P('bin'), may hold values 0 or 1
- group_ids: int32 [6144, 1], replicated, may hold values from 0 to 10
- group_weight: float32 [11], replicated, may hold values from 0.25 to 4
Outputs:
- prediction: bfloat16 [32768, 6144], P('bin', 'trk')
- head_grad: float32 [768, 6144], P('bin', 'trk')
- feature_grad: bfloat16 [32768, 768], P(('bin', 'trk'))
Inputs may be any that keep to these rules, and one draw needn't show every extreme that they name: `group_ids`: every group id is held by at least one track.
All inputs are finite; a program needn't handle non-finite values. No bound on the sum of `missing` on one device may be relied on, other than what follows from the above.
Results may differ from a plain program's by a relative error of at most 0.019.
Values may be sent and summed in bfloat16 or wider, within the bound.
No kernel may reach another device: no remote copies, remote signals or barrier semaphores. Data moves between devices by JAX's collectives and lax.ppermute only.
A program may use at most 128 MiB of HBM per device.

v0:
```python
import math
import jax
import jax.numpy as jnp
from jax import lax
from jax.sharding import PartitionSpec as P

logit_cap = 20.0


def padded_2(value, sides, width):
    for axis, dim in sides:
        size, length = (lax.axis_size(axis), value.shape[dim])
        up = [(i, (i + 1) % size) for i in range(size - 1)]
        down = [(j, i) for i, j in up]
        last = lax.slice_in_dim(value, length - width, length, axis=dim)
        initial = lax.slice_in_dim(value, 0, width, axis=dim)
        before = lax.ppermute(last, axis, up)
        after = lax.ppermute(initial, axis, down)
        value = jnp.concatenate([before, value, after], axis=dim)
    return value


def attend_block(state_pair, queries, key_block, value_block, score_scale):
    numerator, denominator = state_pair
    scores = (
        jnp.einsum("rhd,nd->rhn", queries, key_block, preferred_element_type=jnp.float32)
        * score_scale
    )
    scores = logit_cap * jnp.tanh(scores / logit_cap)
    exp_weights = jnp.exp(scores)
    numerator = numerator + jnp.einsum(
        "rhn,nd->rhd",
        exp_weights.astype(jnp.bfloat16),
        value_block,
        preferred_element_type=jnp.float32,
    )
    denominator = denominator + jnp.sum(exp_weights, axis=2)
    return (numerator, denominator)


def make_folder(queries, head_dim):
    score_scale = 1.0 / math.sqrt(head_dim)

    def fold(accum, key_piece, offset):
        piece_rows = key_piece.shape[0]
        block_rows = math.gcd(piece_rows, 2048)
        stacked = key_piece.reshape(piece_rows // block_rows, block_rows, key_piece.shape[1])

        def fold_step(running, one_block):
            updated = attend_block(
                running, queries, one_block[:, :head_dim], one_block[:, head_dim:], score_scale
            )
            return (updated, None)

        result, _ = lax.scan(fold_step, accum, stacked)
        return result

    return fold


def body(
    trunk,
    norm_gain,
    w_query,
    w_kv,
    w_out,
    w_up,
    skip,
    conv_w,
    head_w,
    head_bias,
    targets,
    missing,
    group_ids,
    group_weight,
):
    row_count = trunk.shape[0]
    head_dim = w_kv.shape[1] // 2
    head_count = w_query.shape[1] // head_dim
    widened = trunk.astype(jnp.float32)
    meansq = jnp.mean(widened * widened, axis=1, keepdims=True)
    normed = (widened * lax.rsqrt(meansq + 1e-06) * norm_gain).astype(jnp.bfloat16)
    queries = (
        jnp.dot(normed, w_query, preferred_element_type=jnp.float32)
        .astype(jnp.bfloat16)
        .reshape(row_count, head_count, head_dim)
    )
    keyvals = jnp.dot(normed, w_kv, preferred_element_type=jnp.float32).astype(jnp.bfloat16)
    start_pair = (
        jnp.zeros((row_count, head_count, head_dim), jnp.float32),
        jnp.zeros((row_count, head_count), jnp.float32),
    )
    folder = make_folder(queries, head_dim)
    numerator, denominator = folder(
        start_pair, lax.all_gather(keyvals, ("bin", "trk"), axis=0, tiled=True), jnp.int32(0)
    )
    attended = (
        (numerator / denominator[:, :, None])
        .astype(jnp.bfloat16)
        .reshape(row_count, head_count * head_dim)
    )
    hidden = (widened + jnp.dot(attended, w_out, preferred_element_type=jnp.float32)).astype(
        jnp.bfloat16
    )
    upward = jnp.dot(hidden, w_up, preferred_element_type=jnp.float32)
    factor = skip.shape[0] // row_count
    upsampled = (jnp.repeat(upward, factor, axis=0) + skip.astype(jnp.float32)).astype(jnp.bfloat16)
    tap_count = conv_w.shape[0]
    rim_width = tap_count // 2
    padded = padded_2(upsampled, ((("bin", "trk"), 0),), rim_width)
    pos_count = upsampled.shape[0]
    windows = jnp.concatenate([padded[tap : tap + pos_count] for tap in range(tap_count)], axis=1)
    kernel_flat = conv_w.reshape(tap_count * conv_w.shape[1], conv_w.shape[2])
    conved = jnp.dot(windows, kernel_flat, preferred_element_type=jnp.float32)
    feature = (upsampled.astype(jnp.float32) + jax.nn.gelu(conved)).astype(jnp.bfloat16)
    panel_feat = lax.all_gather(feature, "trk", axis=0, tiled=True)
    logits = jnp.dot(panel_feat, head_w, preferred_element_type=jnp.float32) + head_bias
    smooth = jax.nn.softplus(logits)
    prediction = smooth.astype(jnp.bfloat16)
    tile_width = head_w.shape[1]
    groups = group_weight.shape[0]
    total_tracks = group_ids.shape[0]
    labels = jnp.arange(groups, dtype=jnp.int32)
    counts = jnp.sum((group_ids == labels[None, :]).astype(jnp.int32), axis=0)
    per_group = group_weight * total_tracks / (groups * counts.astype(jnp.float32))
    local_ids = lax.dynamic_slice_in_dim(
        group_ids, lax.axis_index("trk") * tile_width, tile_width, 0
    )
    track_scale = jnp.sum(jnp.where(local_ids == labels[None, :], per_group[None, :], 0.0), axis=1)
    keep_mask = 1.0 - jnp.repeat(missing.astype(jnp.float32), factor)[:, None]
    misfit = smooth - targets.astype(jnp.float32)
    slope_grad = (keep_mask * track_scale[None, :] * misfit * jax.nn.sigmoid(logits)).astype(
        jnp.bfloat16
    )
    positions = panel_feat.shape[0] * lax.axis_size("bin")
    product = lax.dot_general(
        panel_feat, slope_grad, (((0,), (0,)), ((), ())), preferred_element_type=jnp.float32
    )
    head_grad = lax.psum_scatter(
        (product / positions).astype(jnp.bfloat16), "bin", scatter_dimension=0, tiled=True
    ).astype(jnp.float32)
    partial_value = lax.dot_general(
        slope_grad, head_w, (((1,), (1,)), ((), ())), preferred_element_type=jnp.float32
    )
    feature_grad = lax.psum_scatter(
        partial_value.astype(jnp.bfloat16), "trk", scatter_dimension=0, tiled=True
    )
    return (prediction, head_grad, feature_grad)


def solution(mesh):
    in_specs = (
        P(("bin", "trk"), None),
        P(),
        P(),
        P(),
        P(),
        P(),
        P(("bin", "trk"), None),
        P(),
        P(None, "trk"),
        P("trk"),
        P("bin", "trk"),
        P("bin"),
        P(),
        P(),
    )
    out_specs = (P("bin", "trk"), P("bin", "trk"), P(("bin", "trk"), None))
    return jax.shard_map(body, mesh=mesh, in_specs=in_specs, out_specs=out_specs, check_vma=False)
```

profile of v0, /device:TPU:0, one launch (start us, length us, event | category | flops | bytes accessed | tf_op | source)
XLA Modules:
  0.0 599.8 jit_solution(18380595523179321211)
XLA Ops:
  7.2 1.2 fusion.20
  8.5 2.2 convolution_convert_fusion.2
  10.7 1.6 fusion.5
  12.4 306.4 %all-gather.3.cloned.1.call-done = bf16[8192,256]{1,0:T(8,128)(2,1)} async-done(((bf16[64,256]{1,0:T(8,128)(2,1)}), bf16[8192,256]{1,0:T(8,128)(2,1)}) %all-gather.3.cloned.1.call-update) | async-done | bytes 4194320 | tf_op jit(solution)/shard_map/all_gather | solution.py:95
  318.8 22.4 %while.15 = (s32[]{:T(128)}, f32[64,8,128]{2,0,1:T(8,128)S(1)}, f32[64,8]{0,1:T(8,128)S(1)}, bf16[4,2048,256]{2,1,0:T(8,128)(2,1)}, bf16[64,8,128]{2,0,1:T(8,128)(2,1)S(1)}, /*index=5*/s32[]{:T(128)}, s32[]{:T(128)}) while((s32[]{:T(128)}, f32[64,8,128]{2,0,1:T(8,128)S(1)}, f32[64,8]{0,1:T(8,128)S(1)}, ...), condition=%wide.region_3.4_spmd.clone, body=%wide.region_1.3_spmd.clone.sunk | while | flops 541196800 | bytes 12198016 | solution.py:55
  318.8 2.3 dynamic-slice_bitcast_fusion.2
  321.1 2.5 bitcast_reduce_fusion.2
  323.6 0.8 fusion.56
  324.4 2.3 dynamic-slice_bitcast_fusion.2
  326.7 2.5 bitcast_reduce_fusion.2
  329.2 0.8 fusion.56
  330.0 2.3 dynamic-slice_bitcast_fusion.2
  332.3 2.5 bitcast_reduce_fusion.2
  334.8 0.8 fusion.56
  335.6 2.3 dynamic-slice_bitcast_fusion.2
  337.9 2.5 bitcast_reduce_fusion.2
  341.2 4.4 fusion.4
  345.7 1.9 broadcast_in_dim.34
  347.6 2.3 reshape.46
  349.9 1.3 add_convert_fusion
  351.2 4.5 collective-permute-start
  355.7 1.3 collective-permute-start.1
  357.3 5.4 collective-permute-done.1
  363.0 5.3 fusion.14
  369.2 65.0 %all-gather.5.cloned.1.call-done = bf16[2048,768]{1,0:T(8,128)(2,1)} async-done(((bf16[256,768]{1,0:T(8,128)(2,1)}), bf16[2048,768]{1,0:T(8,128)(2,1)}) %all-gather.5.cloned.1.call-update) | async-done | bytes 3145744 | tf_op jit(solution)/shard_map/all_gather | solution.py:116
  434.2 10.5 %multiply_convert_fusion = (bf16[2048,768]{1,0:T(8,128)(2,1)S(1)}, bf16[2048,768]{1,0:T(8,128)(2,1)}) fusion(bf16[2048,768]{1,0:T(8,128)(2,1)} %param.26, f32[768]{0:T(1024)S(1)} %select_reduce_fusion, f32[2048]{0:T(1024)S(1)} %sub.20, f32[768]{0:T(1024)S(1)} %copy-done.5, bf16[2048,768]{1,0:T(8,128)(2,1)} %all-gather.5.cloned.1.call-done, ...), kind=kOutput, calls=%fused_computation.10 | convolution fusion | flops 2442657792 | bytes 13776896 | tf_op jit(solution)/shard_map/dot_general | solution.py:117
  444.7 1.7 copy-done.7
  446.4 3.7 multiply_convert_fusion.1
  450.2 6.5 %convolution_convert_fusion = bf16[2048,768]{1,0:T(8,128)(2,1)} fusion(bf16[2048,768]{1,0:T(8,128)(2,1)} %copy-done.7, bf16[768,768]{1,0:T(8,128)(2,1)} %param.24), kind=kOutput, calls=%fused_computation.12 | convolution fusion | flops 2417491968 | bytes 7471104 | tf_op jit(solution)/shard_map/dot_general | solution.py:142
  456.7 53.6 %reduce-scatter.3.cloned.1.call-done = bf16[48,768]{1,0:T(8,128)(2,1)} async-done(((bf16[768,768]{1,0:T(8,128)(2,1)}), bf16[48,768]{1,0:T(8,128)(2,1)}) %reduce-scatter.3.cloned.1.call-update) | async-done | bytes 73744 | tf_op jit(solution)/shard_map/reduce_scatter | solution.py:139
  510.4 1.6 convert_element_type.80
  511.9 81.4 %reduce-scatter.5.cloned.1.call-done = bf16[256,768]{1,0:T(8,128)(2,1)} async-done(((bf16[2048,768]{1,0:T(8,128)(2,1)}), bf16[256,768]{1,0:T(8,128)(2,1)}) %reduce-scatter.5.cloned.1.call-update) | async-done | bytes 393232 | tf_op jit(solution)/shard_map/reduce_scatter | solution.py:145
  (52 shorter events, 2.3 us)
Async XLA Ops:
  7.2 3.6 copy-start
  7.2 311.6 %all-gather.3.cloned.1.call-start = ((), (), s32[]{:S(2)}) async-start(), calls=%async_computation.2 | async-start | bytes 4227072 | tf_op jit(solution)/shard_map/all_gather | solution.py:95
  10.7 423.5 %all-gather.5.cloned.1.call-start = ((), (), s32[]{:S(2)}) async-start(), calls=%async_computation.3 | async-start | bytes 3538944 | tf_op jit(solution)/shard_map/all_gather | solution.py:116
  321.1 2.5 copy-start.1
  326.7 2.5 copy-start.1
  332.3 2.5 copy-start.1
  337.9 2.5 copy-start.1
  351.2 5.8 collective-permute-start
  355.7 7.0 %collective-permute-start.1 = (bf16[2,768]{1,0:T(2,128)(2,1)S(1)}, bf16[2,768]{1,0:T(2,128)(2,1)S(1)}, u32[]{:S(2)}, u32[]{:S(2)}) collective-permute-start(bf16[2,768]{1,0:T(2,128)(2,1)S(1)} %get-tuple-element.123), channel_id=1, source_target_pairs={{1,0},{2,1},{3,2},{4,3},{5,4},{6,5},{7,6},{8,7},{9,8},{10,9},{11,1... | collective-permute-start | bytes 9224 | tf_op jit(solution)/shard_map/ppermute | solution.py:18
  363.0 5.6 copy-start.3
  363.0 5.9 copy-start.2
  363.0 6.1 %copy-start.6 = (f32[11]{0:T(128)S(1)}, f32[11]{0:T(128)}, u32[]{:S(2)}) copy-start(f32[11]{0:T(128)} %param.29) | copy-start | bytes 136
  363.0 71.2 %copy-start.5 = (f32[768]{0:T(1024)S(1)}, f32[768]{0:T(1024)}, u32[]{:S(2)}) copy-start(f32[768]{0:T(1024)} %param.25) | copy-start | bytes 9220
  368.3 142.1 %reduce-scatter.3.cloned.1.call-start = ((), (), s32[]{:S(2)}) async-start(), calls=%async_computation.4 | async-start | bytes 1253376 | tf_op jit(solution)/shard_map/reduce_scatter | solution.py:139
  434.2 12.2 %copy-start.4 = (bf16[2048,768]{1,0:T(8,128)(2,1)S(1)}, bf16[2048,768]{1,0:T(8,128)(2,1)}, u32[]{:S(2)}) copy-start(bf16[2048,768]{1,0:T(8,128)(2,1)} %all-gather.5.cloned.1.call-done) | copy-start | bytes 9437188
  444.7 1.7 copy-start.7
  450.1 143.2 %reduce-scatter.5.cloned.1.call-start = ((), (), s32[]{:S(2)}) async-start(), calls=%async_computation.5 | async-start | bytes 3538944 | tf_op jit(solution)/shard_map/reduce_scatter | solution.py:145
Sparse Core Ops, SparseCore 0:
  10.8 307.9 all-gather.2
  368.4 65.7 all-gather.4
  450.2 60.0 reduce-scatter.2
  514.7 78.5 reduce-scatter.4
where the time goes:
time: 600 us
  waiting for transfers between devices  512 us (85%)
  matrix products  47.5 us (8%)
  local copies, waits for them, and re-layouts  15.4 us (3%)
  between operations  14 us (2%)
  starting transfers between devices  6.16 us (1%)
    all_gather x1, waiting for transfers between devices, body(): lax.all_gather(keyvals, ('bin', 'trk'), axis=0, tiled=True)  306 us
    reduce_scatter x1, waiting for transfers between devices, body(): lax.psum_scatter(partial_value.astype(jnp.bfloat16), 'trk', scatter_dimen...  81.4 us
    all_gather x1, waiting for transfers between devices, body(): panel_feat = lax.all_gather(feature, 'trk', axis=0, tiled=True)  65 us
    reduce_scatter x1, waiting for transfers between devices, body(): lax.psum_scatter((product / positions).astype(jnp.bfloat16), 'bin', scatt...  53.6 us
  transfers between devices with their start and end apart: 6, of which 5 were waited for; matrix products, arithmetic and copies ran while one was open for 2% of the time, Pallas kernels for 0%

commit v1 on v0

--- a/solution.py
+++ b/solution.py
@@ -5,6 +5,15 @@
 from jax.sharding import PartitionSpec as P
 
 logit_cap = 20.0
+close_slot = lambda work_x: jnp.concatenate(
+    lax.all_to_all(
+        jnp.stack([work_x for _ in range(lax.psum(1, ("bin", "trk")))], axis=0),
+        ("bin", "trk"),
+        split_axis=0,
+        concat_axis=0,
+    ),
+    axis=0,
+)
 
 
 def padded_2(value, sides, width):
@@ -91,9 +100,7 @@
         jnp.zeros((row_count, head_count), jnp.float32),
     )
     folder = make_folder(queries, head_dim)
-    numerator, denominator = folder(
-        start_pair, lax.all_gather(keyvals, ("bin", "trk"), axis=0, tiled=True), jnp.int32(0)
-    )
+    numerator, denominator = folder(start_pair, close_slot(keyvals), jnp.int32(0))
     attended = (
         (numerator / denominator[:, :, None])
         .astype(jnp.bfloat16)

time: 600 us -> 354 us (0.59)
  waiting for transfers between devices: 512 us -> 252 us
  starting transfers between devices: 6.16 us -> 18.2 us
    all_gather x1 -> x0, waiting for transfers between devices: 306 us -> none  [body(): lax.all_gather(keyvals, ('bin', 'trk'), axis=0, tiled=True)]
    all_to_all x0 -> x1, waiting for transfers between devices: none -> 48.4 us  [lax.all_to_all(jnp.stack([work_x for _ in range(lax.psum(1, ('bin', 'trk'...]
    all_to_all x0 -> x1, starting transfers between devices: none -> 11.7 us  [lax.all_to_all(jnp.stack([work_x for _ in range(lax.psum(1, ('bin', 'trk'...]
  transfers between devices with their start and end apart: 6 -> 6, of which waited for: 5 -> 5; matrix products, arithmetic and copies ran while one was open for 2% -> 3% of each run, Pallas kernels for 0% -> 0%
where the time goes in v1:
time: 354 us
  waiting for transfers between devices  252 us (71%)
  matrix products  46.9 us (13%)
  starting transfers between devices  18.2 us (5%)
  local copies, waits for them, and re-layouts  17.9 us (5%)
  between operations  14 us (4%)
  other arithmetic  4.76 us (1%)
    reduce_scatter x1, waiting for transfers between devices, body(): lax.psum_scatter(partial_value.astype(jnp.bfloat16), 'trk', scatter_dimen...  81.5 us
    all_gather x1, waiting for transfers between devices, body(): panel_feat = lax.all_gather(feature, 'trk', axis=0, tiled=True)  62.9 us
    reduce_scatter x1, waiting for transfers between devices, body(): lax.psum_scatter((product / positions).astype(jnp.bfloat16), 'bin', scatt...  53.6 us
    all_to_all x1, waiting for transfers between devices, lax.all_to_all(jnp.stack([work_x for _ in range(lax.psum(1, ('bin', 'trk'...  48.4 us
    all_to_all x1, starting transfers between devices, lax.all_to_all(jnp.stack([work_x for _ in range(lax.psum(1, ('bin', 'trk'...  11.7 us
    dot_general x1, matrix products, body(): jnp.dot(panel_feat, head_w, preferred_element_type=jnp.float32) + head_bias  10.5 us
    dot_general x4, matrix products, attend_block(): jnp.einsum('rhd,nd->rhn', queries, key_block, preferred_element_type=jnp....  10.2 us
    squeeze x4, local copies, waits for them, and re-layouts, fold(): result, _ = lax.scan(fold_step, accum, stacked)  9.06 us
  transfers between devices with their start and end apart: 6, of which 5 were waited for; matrix products, arithmetic and copies ran while one was open for 3% of the time, Pallas kernels for 0%

profile of v1, /device:TPU:0, one launch (start us, length us, event | category | flops | bytes accessed | tf_op | source)
XLA Modules:
  0.0 353.7 jit_solution(3387256162302402909)
XLA Ops:
  7.2 1.2 fusion.20
  8.4 1.6 convolution_convert_fusion.2
  10.0 2.5 stack.2
  12.5 11.7 %all-to-all-start = ((bf16[128,64,256]{2,1,0:T(8,128)(2,1)}), bf16[128,64,256]{2,1,0:T(8,128)(2,1)}, u32[]{:S(2)}, u32[]{:S(2)}) async-start(bf16[128,64,256]{2,1,0:T(8,128)(2,1)} %stack.2), calls=%async_computation | async-start | bytes 8388608 | tf_op jit(solution)/shard_map/all_to_all | solution.py:9
  24.3 1.6 fusion.5
  25.9 48.4 %all-to-all-done = bf16[128,64,256]{2,1,0:T(8,128)(2,1)} async-done(((bf16[128,64,256]{2,1,0:T(8,128)(2,1)}), bf16[128,64,256]{2,1,0:T(8,128)(2,1)}, u32[]{:S(2)}, u32[]{:S(2)}) %all-to-all-start) | async-done | bytes 4194336 | tf_op jit(solution)/shard_map/all_to_all | solution.py:9
  74.3 22.4 %while.15 = (s32[]{:T(128)}, f32[64,8,128]{2,0,1:T(8,128)S(1)}, f32[64,8]{0,1:T(8,128)S(1)}, bf16[4,2048,256]{2,1,0:T(8,128)(2,1)}, bf16[64,8,128]{2,0,1:T(8,128)(2,1)S(1)}, /*index=5*/s32[]{:T(128)}, s32[]{:T(128)}) while((s32[]{:T(128)}, f32[64,8,128]{2,0,1:T(8,128)S(1)}, f32[64,8]{0,1:T(8,128)S(1)}, ...), condition=%wide.region_3.4_spmd.clone, body=%wide.region_1.3_spmd.clone.sunk | while | flops 541196800 | bytes 12198016 | solution.py:64
  74.3 2.3 dynamic-slice_bitcast_fusion.2
  76.6 2.5 bitcast_reduce_fusion.2
  79.1 0.8 fusion.56
  79.9 2.3 dynamic-slice_bitcast_fusion.2
  82.2 2.5 bitcast_reduce_fusion.2
  85.5 2.3 dynamic-slice_bitcast_fusion.2
  87.8 2.5 bitcast_reduce_fusion.2
  91.1 2.3 dynamic-slice_bitcast_fusion.2
  93.4 2.5 bitcast_reduce_fusion.2
  96.7 4.4 %fusion.4 = f32[64,768]{1,0:T(8,128)} fusion(bf16[1536,768]{1,0:T(8,128)(2,1)} %param.21, bf16[1024,1536]{1,0:T(8,128)(2,1)} %param.20, bf16[64,1536]{1,0:T(8,128)(2,1)} %param.16, f32[64,8,128]{2,0,1:T(8,128)S(1)} %get-tuple-element.69, f32[64,8]{0,1:T(8,128)S(1)} %get-tuple-element.70), kind=kOutput, calls=%fused_computation.17 | convolution fusion | flops 352747520 | bytes 6162432 | tf_op jit(solution)/shard_map/dot_general | solution.py:112
  101.2 1.9 broadcast_in_dim.34
  103.1 2.3 reshape.44
  105.4 1.3 add_convert_fusion
  106.7 4.9 %collective-permute-start = (bf16[2,768]{1,0:T(2,128)(2,1)S(1)}, bf16[2,768]{1,0:T(2,128)(2,1)S(1)}, u32[]{:S(2)}, u32[]{:S(2)}) collective-permute-start(bf16[2,768]{1,0:T(2,128)(2,1)S(1)} %get-tuple-element.124), channel_id=1, source_target_pairs={{0,1},{1,2},{2,3},{3,4},{4,5},{5,6},{6,7},{7,8},{8,9},{9,10},{10,1... | collective-permute-start | bytes 9224 | tf_op jit(solution)/shard_map/ppermute | solution.py:26
  111.6 1.3 collective-permute-start.1
  113.2 5.4 %collective-permute-done.1 = bf16[2,768]{1,0:T(2,128)(2,1)S(1)} collective-permute-done((bf16[2,768]{1,0:T(2,128)(2,1)S(1)}, bf16[2,768]{1,0:T(2,128)(2,1)S(1)}, u32[]{:S(2)}, u32[]{:S(2)}) %collective-permute-start.1) | collective-permute-done | bytes 3104 | tf_op jit(solution)/shard_map/ppermute | solution.py:27
  118.9 5.3 %fusion.14 = bf16[256,768]{1,0:T(8,128)(2,1)} fusion(bf16[256,768]{1,0:T(8,128)(2,1)S(1)} %add_convert_fusion, bf16[256,3840]{1,0:T(8,128)(2,1)S(1)} %fusion.23, bf16[3840,768]{1,0:T(8,128)(2,1)} %bitcast.63), kind=kOutput, calls=%fused_computation.29 | convolution fusion | flops 1512112128 | bytes 8650752 | tf_op jit(solution)/shard_map/dot_general | solution.py:121
  125.1 62.9 %all-gather.2.cloned.1.call-done = bf16[2048,768]{1,0:T(8,128)(2,1)} async-done(((bf16[256,768]{1,0:T(8,128)(2,1)}), bf16[2048,768]{1,0:T(8,128)(2,1)}) %all-gather.2.cloned.1.call-update) | async-done | bytes 3145744 | tf_op jit(solution)/shard_map/all_gather | solution.py:123
  188.0 10.5 %multiply_convert_fusion = (bf16[2048,768]{1,0:T(8,128)(2,1)S(1)}, bf16[2048,768]{1,0:T(8,128)(2,1)}) fusion(bf16[2048,768]{1,0:T(8,128)(2,1)} %param.26, f32[768]{0:T(1024)S(1)} %select_reduce_fusion, f32[2048]{0:T(1024)S(1)} %sub.20, f32[768]{0:T(1024)S(1)} %copy-done.6, bf16[2048,768]{1,0:T(8,128)(2,1)} %all-gather.2.cloned.1.call-done, ...), kind=kOutput, calls=%fused_computation.10 | convolution fusion | flops 2442657792 | bytes 13776896 | tf_op jit(solution)/shard_map/dot_general | solution.py:124
  198.5 1.7 copy-done.8
  200.1 3.7 %multiply_convert_fusion.1 = bf16[768,768]{1,0:T(8,128)(2,1)} fusion(bf16[2048,768]{1,0:T(8,128)(2,1)S(1)} %copy-done.5, bf16[2048,768]{1,0:T(8,128)(2,1)S(1)} %get-tuple-element.121), kind=kOutput, calls=%fused_computation.13 | convolution fusion | flops 2417098752 | bytes 7471104 | tf_op jit(solution)/shard_map/dot_general | solution.py:143
  203.9 6.5 %convolution_convert_fusion = bf16[2048,768]{1,0:T(8,128)(2,1)} fusion(bf16[2048,768]{1,0:T(8,128)(2,1)} %copy-done.8, bf16[768,768]{1,0:T(8,128)(2,1)} %param.24), kind=kOutput, calls=%fused_computation.12 | convolution fusion | flops 2417491968 | bytes 7471104 | tf_op jit(solution)/shard_map/dot_general | solution.py:149
  210.5 53.6 %reduce-scatter.3.cloned.1.call-done = bf16[48,768]{1,0:T(8,128)(2,1)} async-done(((bf16[768,768]{1,0:T(8,128)(2,1)}), bf16[48,768]{1,0:T(8,128)(2,1)}) %reduce-scatter.3.cloned.1.call-update) | async-done | bytes 73744 | tf_op jit(solution)/shard_map/reduce_scatter | solution.py:146
  264.1 1.6 convert_element_type.80
  265.6 81.5 %reduce-scatter.5.cloned.1.call-done = bf16[256,768]{1,0:T(8,128)(2,1)} async-done(((bf16[2048,768]{1,0:T(8,128)(2,1)}), bf16[256,768]{1,0:T(8,128)(2,1)}) %reduce-scatter.5.cloned.1.call-update) | async-done | bytes 393232 | tf_op jit(solution)/shard_map/reduce_scatter | solution.py:152
  (54 shorter events, 3.7 us)
Async XLA Ops:
  7.2 17.1 %copy-start = (bf16[1536,1024]{1,0:T(8,128)(2,1)S(1)}, bf16[1536,1024]{1,0:T(8,128)(2,1)}, u32[]{:S(2)}) copy-start(bf16[1536,1024]{1,0:T(8,128)(2,1)} %param.18) | copy-start | bytes 9437188
  12.5 11.8 %copy-start.2 = (f32[1536]{0:T(1024)S(1)}, f32[1536]{0:T(1024)}, u32[]{:S(2)}) copy-start(f32[1536]{0:T(1024)} %param.17) | copy-start | bytes 18436
  12.5 61.8 %all-to-all-start = ((bf16[128,64,256]{2,1,0:T(8,128)(2,1)}), bf16[128,64,256]{2,1,0:T(8,128)(2,1)}, u32[]{:S(2)}, u32[]{:S(2)}) async-start(bf16[128,64,256]{2,1,0:T(8,128)(2,1)} %stack.2), calls=%async_computation | async-start | bytes 8388608 | tf_op jit(solution)/shard_map/all_to_all | solution.py:9
  24.2 163.8 %all-gather.2.cloned.1.call-start = ((), (), s32[]{:S(2)}) async-start(), calls=%async_computation.3 | async-start | bytes 3538944 | tf_op jit(solution)/shard_map/all_gather | solution.py:123
  76.6 2.6 copy-start.1
  82.2 2.5 copy-start.1
  87.8 2.5 copy-start.1
  93.4 2.5 copy-start.1
  106.7 6.2 %collective-permute-start = (bf16[2,768]{1,0:T(2,128)(2,1)S(1)}, bf16[2,768]{1,0:T(2,128)(2,1)S(1)}, u32[]{:S(2)}, u32[]{:S(2)}) collective-permute-start(bf16[2,768]{1,0:T(2,128)(2,1)S(1)} %get-tuple-element.124), channel_id=1, source_target_pairs={{0,1},{1,2},{2,3},{3,4},{4,5},{5,6},{6,7},{7,8},{8,9},{9,10},{10,1... | collective-permute-start | bytes 9224 | tf_op jit(solution)/shard_map/ppermute | solution.py:26
  111.6 7.0 %collective-permute-start.1 = (bf16[2,768]{1,0:T(2,128)(2,1)S(1)}, bf16[2,768]{1,0:T(2,128)(2,1)S(1)}, u32[]{:S(2)}, u32[]{:S(2)}) collective-permute-start(bf16[2,768]{1,0:T(2,128)(2,1)S(1)} %get-tuple-element.123), channel_id=1, source_target_pairs={{1,0},{2,1},{3,2},{4,3},{5,4},{6,5},{7,6},{8,7},{9,8},{10,9},{11,1... | collective-permute-start | bytes 9224 | tf_op jit(solution)/shard_map/ppermute | solution.py:27
  118.8 5.6 %copy-start.4 = (s32[512]{0:T(512)S(1)}, s32[512]{0:T(512)}, u32[]{:S(2)}) copy-start(s32[512]{0:T(512)} %param.27) | copy-start | bytes 6148
  118.8 5.9 %copy-start.3 = (s32[6144,1]{0,1:T(1,128)S(1)}, s32[6144,1]{0,1:T(1,128)}, u32[]{:S(2)}) copy-start(s32[6144,1]{0,1:T(1,128)} %param.28) | copy-start | bytes 73732
  118.9 6.1 %copy-start.7 = (f32[11]{0:T(128)S(1)}, f32[11]{0:T(128)}, u32[]{:S(2)}) copy-start(f32[11]{0:T(128)} %param.29) | copy-start | bytes 136
  118.9 69.1 %copy-start.6 = (f32[768]{0:T(1024)S(1)}, f32[768]{0:T(1024)}, u32[]{:S(2)}) copy-start(f32[768]{0:T(1024)} %param.25) | copy-start | bytes 9220
  124.2 139.9 %reduce-scatter.3.cloned.1.call-start = ((), (), s32[]{:S(2)}) async-start(), calls=%async_computation.4 | async-start | bytes 1253376 | tf_op jit(solution)/shard_map/reduce_scatter | solution.py:146
  187.9 12.2 %copy-start.5 = (bf16[2048,768]{1,0:T(8,128)(2,1)S(1)}, bf16[2048,768]{1,0:T(8,128)(2,1)}, u32[]{:S(2)}) copy-start(bf16[2048,768]{1,0:T(8,128)(2,1)} %all-gather.2.cloned.1.call-done) | copy-start | bytes 9437188
  198.5 1.7 copy-start.8
  203.9 143.3 %reduce-scatter.5.cloned.1.call-start = ((), (), s32[]{:S(2)}) async-start(), calls=%async_computation.5 | async-start | bytes 3538944 | tf_op jit(solution)/shard_map/reduce_scatter | solution.py:152
Sparse Core Ops, SparseCore 0:
  124.3 63.5 all-gather.1
  204.0 60.0 reduce-scatter.2
  268.6 78.5 reduce-scatter.4
